TPU v7x, 128 devices: a whole 4x4x4 slice. The times are simulated.
128 devices in a mesh: front: 8 (over z, core), panel: 16 (over x, y).
Axes of the slice: x: 4, y: 4, z: 4, core: 2. Of those that a mesh axis runs over, the one named last changes fastest.
Arguments:
- pivot_columns: float32 [8, 8192, 1024], P('front', 'panel')
- child_rows: bfloat16 [8, 16, 16, 4, 8192], P('front', 'panel'), may hold values from -0.375 to 0.375
- slot_rows: int32 [8, 16, 16, 4], P('front', 'panel'), may hold values from -1 to 511, as said below
- parents: int32 [8], replicated, may hold values from 0 to 7, as said below
- pivot_rhs: float32 [8, 1024, 128], P('front'), may hold values from -6 to 6
- boundary_solution: float32 [8, 8192, 128], P('front', 'panel'), may hold values from -6 to 6
Outputs:
- panel_factor: float32 [8, 8192, 1024], P('front', 'panel')
- update_matrix: bfloat16 [8, 8192, 7168], P('front', 'panel')
- front_solution: float32 [8, 8192, 128], P('front', 'panel')
- child_solution: float32 [8, 16, 16, 4, 128], P('front', 'panel')
Inputs may be any that keep to these rules, and one draw needn't show every extreme that they name: parents[c] is the front of this level into which child front c's rows are added; a front may take several children or none. `slot_rows`: the live slots of each tile of 4 slots come first; the rows that one child front sends to one destination device are distinct; for each child front one destination device receives full tiles from every source device.
All inputs are finite; a program needn't handle non-finite values.
Results may differ from a plain program's by a relative error of at most 0.007.
Values may be sent and summed in bfloat16 or wider, within the bound.
A program may use at most 192 MiB of HBM per device.

v0:
```python
import jax
import jax.numpy as jnp
from jax import lax
from jax.sharding import PartitionSpec as P

K = 512
NSTEP = 2


def spread(shard, axis, root):
    mine = lax.axis_index(axis) == root
    return lax.psum(jnp.where(mine, shard, jnp.zeros_like(shard)), axis)


def outer_rows(mine, piece):
    return lax.dot_general(
        mine, piece, (((1,), (1,)), ((), ())), preferred_element_type=jnp.float32
    )


def scatter_term(slots, rows, local_ids, width):
    onehot = (slots.reshape(-1)[None, :] == local_ids[:, None]).astype(jnp.bfloat16)
    return jnp.dot(onehot, rows.reshape(-1, width), preferred_element_type=jnp.float32)


def on_device(pivot_columns, child_rows, slot_rows, parents, pivot_rhs, boundary_solution):
    highest = lax.Precision.HIGHEST
    panel_index = lax.axis_index("panel")
    front_index = lax.axis_index("front")
    piv_cols = pivot_columns[0]
    row_count = piv_cols.shape[0]
    pivots = piv_cols.shape[1]
    width = child_rows.shape[-1]
    rhs_count = pivot_rhs.shape[-1]
    local_ids = jnp.arange(row_count, dtype=jnp.int32)
    glob_rows = panel_index * row_count + local_ids
    rows_out = child_rows[0, 0]
    slots_out = slot_rows[0, 0]
    routed_rows, routed_slots = (
        lax.all_to_all(rows_out, "panel", split_axis=0, concat_axis=0, tiled=True),
        lax.all_to_all(slots_out, "panel", split_axis=0, concat_axis=0, tiled=True),
    )
    piece_rows = lax.all_gather(routed_rows[None], "front", axis=0, tiled=True)
    piece_slots = lax.all_gather(routed_slots[None], "front", axis=0, tiled=True)
    keeping = parents == front_index

    def add_rows(current):
        kept_slots = jnp.where(keeping[:, None, None], piece_slots, -1)
        return scatter_term(kept_slots, piece_rows, local_ids, width)

    def keep_same(current):
        return current

    assembled = lax.cond(
        jnp.any(keeping), add_rows, keep_same, jnp.zeros((row_count, width), jnp.float32)
    )
    work = assembled + jnp.concatenate(
        [piv_cols, jnp.zeros((row_count, width - pivots), jnp.float32)], axis=1
    )
    identity_block = jnp.eye(K, dtype=jnp.float32)

    def factor_block(values):
        lower = jnp.linalg.cholesky(values)
        return lax.linalg.triangular_solve(lower, identity_block, left_side=True, lower=True)

    def empty_block(values):
        return jnp.zeros_like(values)

    factors = []
    inverses = []
    for panel_step in range(NSTEP):
        low_edge = panel_step * K
        high_edge = low_edge + K
        root_rank = low_edge // row_count
        offset = low_edge - root_rank * row_count
        pivot_block = work[offset : offset + K, low_edge:high_edge]
        inverse = lax.cond(panel_index == root_rank, factor_block, empty_block, pivot_block)
        inverse = spread(inverse, "panel", root_rank)
        column = jnp.dot(work[:, low_edge:high_edge], inverse.T, precision=highest)
        column = jnp.where(glob_rows[:, None] >= low_edge, column, 0.0)
        packed = column.astype(jnp.bfloat16)
        factors.append(column)
        inverses.append(inverse)
        work = work - outer_rows(packed, lax.all_gather(packed, "panel", axis=0, tiled=True))
    factor_all = jnp.concatenate(factors, axis=1)
    trailing = work[:, pivots:]
    update_matrix = jnp.where(glob_rows[:, None] >= pivots, trailing, 0.0).astype(jnp.bfloat16)
    known = boundary_solution[0]
    right_side = pivot_rhs[0]

    def local_values(solved):
        extended = jnp.concatenate([solved, jnp.zeros((row_count, rhs_count), jnp.float32)], axis=0)
        begin = jnp.minimum(panel_index * row_count, pivots)
        segment = lax.dynamic_slice_in_dim(extended, begin, row_count)
        return jnp.where(glob_rows[:, None] < pivots, segment, known)

    solved = jnp.zeros((pivots, rhs_count), jnp.float32)
    contract_rows = (((0,), (0,)), ((), ()))
    for panel_step in reversed(range(NSTEP)):
        low_edge = panel_step * K
        high_edge = low_edge + K
        current = local_values(solved)
        masked = jnp.where(glob_rows[:, None] >= high_edge, factors[panel_step], 0.0)
        partial_sum = lax.dot_general(masked, current, contract_rows, precision=highest)
        carried = lax.psum(partial_sum, "panel")
        value = lax.dot_general(
            inverses[panel_step],
            right_side[low_edge:high_edge] - carried,
            contract_rows,
            precision=highest,
        )
        solved = solved.at[low_edge:high_edge].set(value)
    front_values = local_values(solved)
    slot_onehot = (routed_slots[..., None] == local_ids).astype(jnp.float32)
    piece = lax.all_gather(front_values[None], "front", axis=0, tiled=True)
    piece_count = piece.shape[0]
    weights = (jnp.arange(piece_count, dtype=jnp.int32) == parents[front_index]).astype(jnp.float32)
    chosen = jnp.einsum("n,nrh->rh", weights, piece, precision=highest)
    slot_values = jnp.einsum("psr,rh->psh", slot_onehot, chosen, precision=highest)
    child_values = lax.all_to_all(slot_values, "panel", split_axis=0, concat_axis=0, tiled=True)
    return (factor_all[None], update_matrix[None], front_values[None], child_values[None, None])


def solution(mesh):
    in_specs = (
        P("front", "panel", None),
        P("front", "panel", None, None, None),
        P("front", "panel", None, None),
        P(),
        P("front", None, None),
        P("front", "panel", None),
    )
    out_specs = (
        P("front", "panel", None),
        P("front", "panel", None),
        P("front", "panel", None),
        P("front", "panel", None, None, None),
    )
    return jax.shard_map(
        on_device, mesh=mesh, in_specs=in_specs, out_specs=out_specs, check_vma=False
    )
```

profile of v0, /device:TPU:0, one launch (start us, length us, event | category | flops | bytes accessed | tf_op | source)
XLA Modules:
  0.0 1002.9 jit_solution(4517287727802942974)
XLA Ops:
  7.2 24.1 %all_to_all.19 = bf16[16,4,8192]{2,1,0:T(4,128)(2,1)} all-to-all(bf16[16,4,8192]{2,1,0:T(4,128)(2,1)} %bitcast.145), channel_id=1, replica_groups=mesh['front'=8,'panel'=16] {'panel'}, dimensions={0} | all-to-all | bytes 2097152 | tf_op jit(solution)/shard_map/all_to_all | solution.py:40
  44.0 14.0 %all-gather = s32[128,1,4]{2,1,0:T(1,128)S(1)} all-gather(s32[16,1,4]{2,1,0:T(1,128)S(1)} %all-to-all-done), channel_id=2, replica_groups=mesh['front'=8,'panel'=16] {'front'}, dimensions={0}, use_global_device_ids=true | all-gather | bytes 2304 | tf_op jit(solution)/shard_map/all_gather | solution.py:44
  58.0 22.9 %all-gather.12.cloned.1.call-done = bf16[128,4,8192]{2,1,0:T(4,128)(2,1)} async-done(((bf16[16,4,8192]{2,1,0:T(4,128)(2,1)}), bf16[128,4,8192]{2,1,0:T(4,128)(2,1)}) %all-gather.12.cloned.1.call-update) | async-done | bytes 8388624 | tf_op jit(solution)/shard_map/all_gather | solution.py:43
  80.9 24.2 %conditional.3 = (f32[512,8192]{1,0:T(8,128)}) conditional(s32[]{:T(128)} %convert_element_type.26, () %tuple.36, (pred[8]{0:T(512)(128)(4,1)S(1)}, s32[8,16,4]{2,1,0:T(8,128)S(1)}, s32[512]{0:T(512)S(1)}, bf16[8,16,4,8192]{3,2,1,0:T(4,128)(2,1)}) %tuple.137), branch_computations={%region_1.0_spmd, %region_2.3_spmd} | conditional | flops 4295229952 | bytes 41955344 | solution.py:54
  81.0 12.5 %reshape.120 = bf16[512,8192]{1,0:T(8,128)(2,1)} reshape(bf16[8,16,4,8192]{3,2,1,0:T(4,128)(2,1)} %get-tuple-element.54) | data formatting | bytes 16777216 | tf_op jit(solution)/shard_map/cond/branch_1_fun/reshape | solution.py:23
  93.6 11.5 %fusion = f32[512,8192]{1,0:T(8,128)} fusion(bf16[512,8192]{1,0:T(8,128)(2,1)} %reshape.120, s32[512]{0:T(512)S(1)} %eq.3, s32[512]{0:T(512)S(1)} %get-tuple-element.53), kind=kOutput, calls=%fused_computation | convolution fusion | flops 4295229440 | bytes 25169920 | tf_op jit(solution)/shard_map/cond/branch_1_fun/dot_general | solution.py:23
  117.8 141.4 %conditional.4 = (f32[512,512]{0,1:T(8,128)}) conditional(s32[]{:T(128)} %convert_element_type.27, () %tuple.38, (f32[512,512]{1,0:T(8,128)S(1)}, f32[512,512]{1,0:T(8,128)S(1)}) %tuple.39), branch_computations={%region_3.4_spmd, %region_4.15_spmd} | conditional | flops 1412760064 | bytes 26743068 | solution.py:77
  119.7 11.7 %cholesky.286 = f32[128,128]{1,0:T(8,128)S(1)} custom-call(f32[128,128]{1,0:T(8,128)S(1)} %cholesky.426), custom_call_target="Cholesky" | custom-call | tf_op jit(solution)/shard_map/cond/branch_1_fun/jit(cholesky)/cholesky | solution.py:63
  131.4 9.8 custom-call.27
  143.9 11.7 %cholesky.305 = f32[128,128]{1,0:T(8,128)S(1)} custom-call(f32[128,128]{1,0:T(8,128)S(1)} %cholesky.430), custom_call_target="Cholesky" | custom-call | tf_op jit(solution)/shard_map/cond/branch_1_fun/jit(cholesky)/cholesky | solution.py:63
  157.7 10.0 %custom-call.28 = f32[1,128,128]{1,2,0:T(8,128)S(1)} custom-call(f32[1,128,128]{2,1,0:T(8,128)S(1)} %get-tuple-element.139), custom_call_target="InvertDiagBlocksLowerTriangular" | custom-call | tf_op jit(solution)/shard_map/cond/branch_1_fun/jit(cholesky)/cholesky | solution.py:63
  169.3 11.7 %cholesky.326 = f32[128,128]{1,0:T(8,128)S(1)} custom-call(f32[128,128]{1,0:T(8,128)S(1)} %cholesky.435), custom_call_target="Cholesky" | custom-call | tf_op jit(solution)/shard_map/cond/branch_1_fun/jit(cholesky)/cholesky | solution.py:63
  182.3 9.8 custom-call.29
  193.6 11.7 %cholesky.343 = f32[128,128]{1,0:T(8,128)S(1)} custom-call(f32[128,128]{1,0:T(8,128)S(1)} %convolution_subtract_fusion.5), custom_call_target="Cholesky" | custom-call | tf_op jit(solution)/shard_map/cond/branch_1_fun/jit(cholesky)/cholesky | solution.py:63
  215.3 39.3 %custom-call.30 = f32[4,128,128]{1,2,0:T(8,128)S(1)} custom-call(f32[4,128,128]{2,1,0:T(8,128)S(1)} %get-tuple-element.77), custom_call_target="InvertDiagBlocksLowerTriangular" | custom-call | tf_op jit(solution)/shard_map/cond/branch_1_fun/triangular_solve/custom-call.3 | solution.py:64
  261.7 82.1 %all-reduce.11.cloned.1.call-done = f32[512,512]{0,1:T(8,128)} async-done(((f32[512,512]{0,1:T(8,128)}), f32[512,512]{0,1:T(8,128)}) %all-reduce.11.cloned.1.call-update) | async-done | bytes 1048592 | tf_op jit(solution)/shard_map/psum | solution.py:12
  348.1 77.5 %all-gather.8.cloned.1.call-done = bf16[8192,512]{0,1:T(8,128)(2,1)} async-done(((bf16[512,512]{0,1:T(8,128)(2,1)}), bf16[8192,512]{0,1:T(8,128)(2,1)}) %all-gather.8.cloned.1.call-update) | async-done | bytes 8388624 | tf_op jit(solution)/shard_map/all_gather | solution.py:84
  425.6 18.7 %convolution_subtract_fusion.12 = f32[512,8192]{1,0:T(8,128)} fusion(f32[512,8192]{1,0:T(8,128)} %copy-done, bf16[512,512]{0,1:T(8,128)(2,1)} %get-tuple-element.163, bf16[8192,512]{0,1:T(8,128)(2,1)} %all-gather.8.cloned.1.call-done), kind=kOutput, calls=%fused_computation.141 | convolution fusion | flops 4299161600 | bytes 42467328 | tf_op jit(solution)/shard_map/dot_general | solution.py:16
  455.1 237.6 %all-reduce.13.cloned.1.call-done = f32[512,512]{0,1:T(8,128)} async-done(((f32[512,512]{0,1:T(8,128)}), f32[512,512]{0,1:T(8,128)}) %all-reduce.13.cloned.1.call-update) | async-done | bytes 1048592 | tf_op jit(solution)/shard_map/psum | solution.py:12
  698.8 83.3 %all-reduce.15.cloned.1.call-done = f32[512,128]{1,0:T(8,128)} async-done(((f32[512,128]{1,0:T(8,128)}), f32[512,128]{1,0:T(8,128)}) %all-reduce.15.cloned.1.call-update) | async-done | bytes 262160 | tf_op jit(solution)/shard_map/psum | solution.py:105
  786.3 83.5 %all-reduce.17.cloned.1.call-done = f32[512,128]{1,0:T(8,128)} async-done(((f32[512,128]{1,0:T(8,128)}), f32[512,128]{1,0:T(8,128)}) %all-reduce.17.cloned.1.call-update) | async-done | bytes 262160 | tf_op jit(solution)/shard_map/psum | solution.py:105
  874.5 23.5 %all-gather.14.cloned.1.call-done = f32[4096,128]{1,0:T(8,128)} async-done(((f32[512,128]{1,0:T(8,128)}), f32[4096,128]{1,0:T(8,128)}) %all-gather.14.cloned.1.call-update) | async-done | bytes 2097168 | tf_op jit(solution)/shard_map/all_gather | solution.py:115
  918.0 60.9 %all-gather.10.cloned.1.call-done = bf16[8192,512]{0,1:T(8,128)(2,1)} async-done(((bf16[512,512]{0,1:T(8,128)(2,1)}), bf16[8192,512]{0,1:T(8,128)(2,1)}) %all-gather.10.cloned.1.call-update) | async-done | bytes 8388624 | tf_op jit(solution)/shard_map/all_gather | solution.py:84
  986.0 9.0 fusion.66
  (112 shorter events, 116.4 us)
Async XLA Ops:
  7.2 73.7 %all-gather.12.cloned.1.call-start = ((), (), s32[]{:S(2)}) async-start(), calls=%async_computation.9 | async-start | bytes 9437184 | tf_op jit(solution)/shard_map/all_gather | solution.py:43
  32.7 11.3 %all-to-all-start = ((s32[16,1,4]{2,1,0:T(1,128)}), s32[16,1,4]{2,1,0:T(1,128)S(1)}, u32[]{:S(2)}, u32[]{:S(2)}) async-start(s32[16,1,4]{2,1,0:T(1,128)} %copy.30), calls=%async_computation | async-start | bytes 16384 | tf_op jit(solution)/shard_map/all_to_all | solution.py:41
  36.5 307.3 %all-reduce.11.cloned.1.call-start = ((), (), s32[]{:S(2)}) async-start(), calls=%async_computation.3 | async-start | bytes 2097152 | tf_op jit(solution)/shard_map/psum | solution.py:12
  112.0 5.7 copy-start
  118.7 1.0 copy-start.2
  261.6 164.0 %all-gather.8.cloned.1.call-start = ((), (), s32[]{:S(2)}) async-start(), calls=%async_computation.4 | async-start | bytes 8912896 | tf_op jit(solution)/shard_map/all_gather | solution.py:84
  348.0 344.7 %all-reduce.13.cloned.1.call-start = ((), (), s32[]{:S(2)}) async-start(), calls=%async_computation.5 | async-start | bytes 2097152 | tf_op jit(solution)/shard_map/psum | solution.py:12
  445.6 251.4 %copy-start.4 = (f32[1,512,128]{2,1,0:T(8,128)S(1)}, f32[1,512,128]{2,1,0:T(8,128)}, u32[]{:S(2)}) copy-start(f32[1,512,128]{2,1,0:T(8,128)} %param.24) | copy-start | bytes 786436
  453.8 328.3 %copy-start.6 = (f32[1,1024,128]{2,1,0:T(8,128)S(1)}, f32[1,1024,128]{2,1,0:T(8,128)}, u32[]{:S(2)}) copy-start(f32[1,1024,128]{2,1,0:T(8,128)} %param.23) | copy-start | bytes 1572868
  453.8 419.9 %copy-start.7 = (s32[8]{0:T(128)S(1)}, s32[8]{0:T(128)}, u32[]{:S(2)}) copy-start(s32[8]{0:T(128)} %param.22) | copy-start | bytes 100
  454.9 327.2 %all-reduce.15.cloned.1.call-start = ((), (), s32[]{:S(2)}) async-start(), calls=%async_computation.7 | async-start | bytes 524288 | tf_op jit(solution)/shard_map/psum | solution.py:105
  698.8 171.0 %all-reduce.17.cloned.1.call-start = ((), (), s32[]{:S(2)}) async-start(), calls=%async_computation.8 | async-start | bytes 524288 | tf_op jit(solution)/shard_map/psum | solution.py:105
  784.4 194.4 %copy-start.1 = (bf16[512,512]{0,1:T(8,128)(2,1)S(1)}, bf16[512,512]{0,1:T(8,128)(2,1)}, u32[]{:S(2)}) copy-start(bf16[512,512]{0,1:T(8,128)(2,1)} %get-tuple-element.165) | copy-start | bytes 1572868
  786.2 111.8 %all-gather.14.cloned.1.call-start = ((), (), s32[]{:S(2)}) async-start(), calls=%async_computation.10 | async-start | bytes 2359296 | tf_op jit(solution)/shard_map/all_gather | solution.py:115
  873.0 105.8 %all-gather.10.cloned.1.call-start = ((), (), s32[]{:S(2)}) async-start(), calls=%async_computation.6 | async-start | bytes 8912896 | tf_op jit(solution)/shard_map/all_gather | solution.py:84
  903.3 14.6 %all-to-all-start.2 = ((f32[16,4,128]{2,1,0:T(4,128)}), f32[16,4,128]{2,1,0:T(4,128)S(1)}, u32[]{:S(2)}, u32[]{:S(2)}) async-start(f32[16,4,128]{2,1,0:T(4,128)} %copy.36), calls=%async_computation.2 | async-start | bytes 65536 | tf_op jit(solution)/shard_map/all_to_all | solution.py:120
Sparse Core Ops, SparseCore 0:
  31.4 49.3 all-gather.11
  261.7 82.0 all-reduce.10
  348.1 77.4 all-gather.7
  455.1 237.5 all-reduce.12
  698.9 83.2 all-reduce.14
  786.3 83.3 all-reduce.16
  873.2 24.8 all-gather.13
  900.1 78.6 all-gather.9
where the time goes:
time: 1010 us; the launch traced here: 1000 us
  waiting for transfers between devices  681 us (67%)
  other arithmetic  142 us (14%)
  matrix products  67.1 us (7%)
  blocking collectives  38.1 us (4%)
  local copies, waits for them, and re-layouts  37.7 us (4%)
  between operations  15.5 us (2%)
  starting transfers between devices  11.3 us (1%)
  loops' own time  10.5 us (1%)
    psum x2, waiting for transfers between devices, spread(): return lax.psum(jnp.where(mine, shard, jnp.zeros_like(shard)), axis)  320 us
    psum x2, waiting for transfers between devices, on_device(): carried = lax.psum(partial_sum, 'panel')  167 us
    all_gather x2, waiting for transfers between devices, on_device(): lax.all_gather(packed, 'panel', axis=0, tiled=True)  138 us
    another operation x14, other arithmetic, factor_block(): lower = jnp.linalg.cholesky(values)  78.6 us
    another operation x5, other arithmetic, factor_block(): lax.linalg.triangular_solve(lower, identity_block, left_side=True, lower=...  40 us
    dot_general x2, matrix products, outer_rows(): lax.dot_general(mine, piece, (((1,), (1,)), ((), ())), preferred_element_...  25.8 us
    all_to_all x1, blocking collectives, on_device(): lax.all_to_all(rows_out, 'panel', split_axis=0, concat_axis=0, tiled=True)  24.1 us
    all_gather x1, waiting for transfers between devices, on_device(): piece = lax.all_gather(front_values[None], 'front', axis=0, tiled=True)  23.5 us
  transfers between devices with their start and end apart: 10, of which 10 were waited for; matrix products, arithmetic and copies ran while one was open for 1% of the time, Pallas kernels for 0%

commit v1 on v0

--- a/solution.py
+++ b/solution.py
@@ -5,6 +5,27 @@
 
 K = 512
 NSTEP = 2
+
+
+def ring_gather(x, axis, dim):
+    size, index, rows = (lax.axis_size(axis), lax.axis_index(axis), x.shape[dim])
+    right = [(i, (i + 1) % size) for i in range(size)]
+    left = [(i, (i - 1) % size) for i in range(size)]
+    whole = jnp.zeros((*x.shape[:dim], size * rows, *x.shape[dim + 1 :]), x.dtype)
+    whole = lax.dynamic_update_slice_in_dim(whole, x, index * rows, axis=dim)
+    from_left = from_right = x
+    halfway = size // 2
+    for step in range(1, halfway + 1):
+        from_left = lax.ppermute(from_left, axis, right)
+        whole = lax.dynamic_update_slice_in_dim(
+            whole, from_left, (index - step) % size * rows, axis=dim
+        )
+        if step < size - halfway:
+            from_right = lax.ppermute(from_right, axis, left)
+            whole = lax.dynamic_update_slice_in_dim(
+                whole, from_right, (index + step) % size * rows, axis=dim
+            )
+    return whole
 
 
 def spread(shard, axis, root):
@@ -81,7 +102,7 @@
         packed = column.astype(jnp.bfloat16)
         factors.append(column)
         inverses.append(inverse)
-        work = work - outer_rows(packed, lax.all_gather(packed, "panel", axis=0, tiled=True))
+        work = work - outer_rows(packed, ring_gather(packed, "panel", 0))
     factor_all = jnp.concatenate(factors, axis=1)
     trailing = work[:, pivots:]
     update_matrix = jnp.where(glob_rows[:, None] >= pivots, trailing, 0.0).astype(jnp.bfloat16)

time: 1010 us -> 1030 us (1.020)
  waiting for transfers between devices: 681 us -> 579 us
  starting transfers between devices: 11.3 us -> 83 us
  local copies, waits for them, and re-layouts: 37.7 us -> 95.8 us
    all_gather x2 -> x0, waiting for transfers between devices: 138 us -> none  [on_device(): lax.all_gather(packed, 'panel', axis=0, tiled=True)]
    ppermute x0 -> x30, waiting for transfers between devices: none -> 79.4 us  [the longest x16 79.1 us: ring_gather(): from_left = lax.ppermute(from_left, axis, right)]
    ppermute x0 -> x30, starting transfers between devices: none -> 71.8 us  [the longest x14 69.4 us: ring_gather(): from_right = lax.ppermute(from_right, axis, left)]
    dynamic_update_slice x0 -> x30, local copies, waits for them, and re-layouts: none -> 45.3 us  [the longest x16 23.3 us: ring_gather(): lax.dynamic_update_slice_in_dim(whole, from_left, (index - step) % size *...]
    all_gather x1, waiting for transfers between devices: 23.5 us -> 0.01 us  [on_device(): piece = lax.all_gather(front_values[None], 'front', axis=0, tiled=True)]
    psum x2, waiting for transfers between devices: 320 us -> 306 us  [spread(): return lax.psum(jnp.where(mine, shard, jnp.zeros_like(shard)), axis)]
  transfers between devices with their start and end apart: 10 -> 38, of which waited for: 10 -> 17; matrix products, arithmetic and copies ran while one was open for 1% -> 8% of each run, Pallas kernels for 0% -> 0%
where the time goes in v1:
time: 1030 us
  waiting for transfers between devices  579 us (56%)
  other arithmetic  143 us (14%)
  local copies, waits for them, and re-layouts  95.8 us (9%)
  starting transfers between devices  83 us (8%)
  matrix products  62.1 us (6%)
  blocking collectives  38.1 us (4%)
  between operations  15.3 us (1%)
  loops' own time  12.1 us (1%)
    psum x2, waiting for transfers between devices, spread(): return lax.psum(jnp.where(mine, shard, jnp.zeros_like(shard)), axis)  306 us
    psum x2, waiting for transfers between devices, on_device(): carried = lax.psum(partial_sum, 'panel')  165 us
    ppermute x16, waiting for transfers between devices, ring_gather(): from_left = lax.ppermute(from_left, axis, right)  79.1 us
    another operation x14, other arithmetic, factor_block(): lower = jnp.linalg.cholesky(values)  78.8 us
    ppermute x14, starting transfers between devices, ring_gather(): from_right = lax.ppermute(from_right, axis, left)  69.4 us
    another operation x5, other arithmetic, factor_block(): lax.linalg.triangular_solve(lower, identity_block, left_side=True, lower=...  40.3 us
    all_to_all x1, blocking collectives, on_device(): lax.all_to_all(rows_out, 'panel', split_axis=0, concat_axis=0, tiled=True)  24.1 us
    dynamic_update_slice x16, local copies, waits for them, and re-layouts, ring_gather(): lax.dynamic_update_slice_in_dim(whole, from_left, (index - step) % size *...  23.3 us
  transfers between devices with their start and end apart: 38, of which 17 were waited for; matrix products, arithmetic and copies ran while one was open for 8% of the time, Pallas kernels for 0%

profile of v1, /device:TPU:0, one launch (start us, length us, event | category | flops | bytes accessed | tf_op | source)
XLA Modules:
  0.0 1027.7 jit_solution(12366379211818486900)
XLA Ops:
  7.2 24.1 %all_to_all.19 = bf16[16,4,8192]{2,1,0:T(4,128)(2,1)} all-to-all(bf16[16,4,8192]{2,1,0:T(4,128)(2,1)} %bitcast.145), channel_id=1, replica_groups=mesh['front'=8,'panel'=16] {'panel'}, dimensions={0} | all-to-all | bytes 2097152 | tf_op jit(solution)/shard_map/all_to_all | solution.py:61
  44.0 14.0 %all-gather = s32[128,1,4]{2,1,0:T(1,128)S(1)} all-gather(s32[16,1,4]{2,1,0:T(1,128)S(1)} %all-to-all-done), channel_id=2, replica_groups=mesh['front'=8,'panel'=16] {'front'}, dimensions={0}, use_global_device_ids=true | all-gather | bytes 2304 | tf_op jit(solution)/shard_map/all_gather | solution.py:65
  58.0 22.9 %all-gather.6.cloned.1.call-done = bf16[128,4,8192]{2,1,0:T(4,128)(2,1)} async-done(((bf16[16,4,8192]{2,1,0:T(4,128)(2,1)}), bf16[128,4,8192]{2,1,0:T(4,128)(2,1)}) %all-gather.6.cloned.1.call-update) | async-done | bytes 8388624 | tf_op jit(solution)/shard_map/all_gather | solution.py:64
  80.9 24.2 %conditional.3 = (f32[512,8192]{1,0:T(8,128)}) conditional(s32[]{:T(128)} %convert_element_type.26, () %tuple.36, (pred[8]{0:T(512)(128)(4,1)S(1)}, s32[8,16,4]{2,1,0:T(8,128)S(1)}, s32[512]{0:T(512)S(1)}, bf16[8,16,4,8192]{3,2,1,0:T(4,128)(2,1)}) %tuple.135), branch_computations={%region_1.0_spmd, %region_2.3_spmd} | conditional | flops 4295229952 | bytes 41955344 | solution.py:75
  81.0 12.5 %reshape.120 = bf16[512,8192]{1,0:T(8,128)(2,1)} reshape(bf16[8,16,4,8192]{3,2,1,0:T(4,128)(2,1)} %get-tuple-element.54) | data formatting | bytes 16777216 | tf_op jit(solution)/shard_map/cond/branch_1_fun/reshape | solution.py:44
  93.6 11.5 %fusion = f32[512,8192]{1,0:T(8,128)} fusion(bf16[512,8192]{1,0:T(8,128)(2,1)} %reshape.120, s32[512]{0:T(512)S(1)} %eq.70, s32[512]{0:T(512)S(1)} %get-tuple-element.53), kind=kOutput, calls=%fused_computation | convolution fusion | flops 4295229440 | bytes 25169920 | tf_op jit(solution)/shard_map/cond/branch_1_fun/dot_general | solution.py:44
  117.9 144.3 %conditional.4 = (f32[512,512]{0,1:T(8,128)}) conditional(s32[]{:T(128)} %convert_element_type.27, () %tuple.38, (f32[512,512]{1,0:T(8,128)S(1)}, f32[512,512]{1,0:T(8,128)S(1)}) %tuple.39), branch_computations={%region_3.4_spmd, %region_4.15_spmd} | conditional | flops 1412760064 | bytes 26744084 | solution.py:98
  119.7 11.7 %cholesky.286 = f32[128,128]{1,0:T(8,128)S(1)} custom-call(f32[128,128]{1,0:T(8,128)S(1)} %cholesky.426), custom_call_target="Cholesky" | custom-call | tf_op jit(solution)/shard_map/cond/branch_1_fun/jit(cholesky)/cholesky | solution.py:84
  131.5 9.8 custom-call.27
  143.9 11.7 %cholesky.305 = f32[128,128]{1,0:T(8,128)S(1)} custom-call(f32[128,128]{1,0:T(8,128)S(1)} %cholesky.430), custom_call_target="Cholesky" | custom-call | tf_op jit(solution)/shard_map/cond/branch_1_fun/jit(cholesky)/cholesky | solution.py:84
  157.7 10.2 custom-call.28
  169.5 11.7 %cholesky.326 = f32[128,128]{1,0:T(8,128)S(1)} custom-call(f32[128,128]{1,0:T(8,128)S(1)} %cholesky.435), custom_call_target="Cholesky" | custom-call | tf_op jit(solution)/shard_map/cond/branch_1_fun/jit(cholesky)/cholesky | solution.py:84
  182.5 9.8 custom-call.29
  193.8 11.7 %cholesky.343 = f32[128,128]{1,0:T(8,128)S(1)} custom-call(f32[128,128]{1,0:T(8,128)S(1)} %convolution_subtract_fusion.5), custom_call_target="Cholesky" | custom-call | tf_op jit(solution)/shard_map/cond/branch_1_fun/jit(cholesky)/cholesky | solution.py:84
  206.9 10.4 %while.6 = (s32[]{:T(128)}, f32[512,512]{1,0:T(8,128)S(1)}, s32[4,2]{0,1:T(2,128)S(1)}, f32[4,128,128]{2,1,0:T(8,128)}, s32[]{:T(128)}) while((s32[]{:T(128)}, f32[512,512]{1,0:T(8,128)S(1)}, s32[4,2]{0,1:T(2,128)S(1)}, f32[4,128,128]{2,1,0:T(8,128)}, s32[]{:T(128)}) %tuple.111), condition=%wide.while_cond.2, body=%wide.while_body.2.sunk | while | flops 2 | bytes 132205 | solution.py:85
  217.4 40.1 %custom-call.30 = f32[4,128,128]{1,2,0:T(8,128)S(1)} custom-call(f32[4,128,128]{2,1,0:T(8,128)} %get-tuple-element.77), custom_call_target="InvertDiagBlocksLowerTriangular" | custom-call | tf_op jit(solution)/shard_map/cond/branch_1_fun/triangular_solve/custom-call.3 | solution.py:85
  264.6 82.1 %all-reduce.11.cloned.1.call-done = f32[512,512]{0,1:T(8,128)} async-done(((f32[512,512]{0,1:T(8,128)}), f32[512,512]{0,1:T(8,128)}) %all-reduce.11.cloned.1.call-update) | async-done | bytes 1048592 | tf_op jit(solution)/shard_map/psum | solution.py:33
  360.4 10.1 collective-permute-done
  467.5 13.9 %convolution_subtract_fusion.12 = f32[512,8192]{1,0:T(8,128)} fusion(f32[512,8192]{1,0:T(8,128)} %copy-done, bf16[512,512]{0,1:T(8,128)(2,1)S(1)} %get-tuple-element.132, bf16[8192,512]{0,1:T(8,128)(2,1)} %constant_dynamic-update-slice_fusion.24), kind=kOutput, calls=%fused_computation.141 | convolution fusion | flops 4299161600 | bytes 42467328 | tf_op jit(solution)/shard_map/dot_general | solution.py:37
  482.7 10.0 conditional.5
  494.0 224.3 %all-reduce.13.cloned.1.call-done = f32[512,512]{0,1:T(8,128)} async-done(((f32[512,512]{0,1:T(8,128)}), f32[512,512]{0,1:T(8,128)}) %all-reduce.13.cloned.1.call-update) | async-done | bytes 1048592 | tf_op jit(solution)/shard_map/psum | solution.py:33
  728.5 83.3 %all-reduce.15.cloned.1.call-done = f32[512,128]{1,0:T(8,128)} async-done(((f32[512,128]{1,0:T(8,128)}), f32[512,128]{1,0:T(8,128)}) %all-reduce.15.cloned.1.call-update) | async-done | bytes 262160 | tf_op jit(solution)/shard_map/psum | solution.py:126
  818.7 81.4 %all-reduce.17.cloned.1.call-done = f32[512,128]{1,0:T(8,128)} async-done(((f32[512,128]{1,0:T(8,128)}), f32[512,128]{1,0:T(8,128)}) %all-reduce.17.cloned.1.call-update) | async-done | bytes 262160 | tf_op jit(solution)/shard_map/psum | solution.py:126
  908.8 10.6 %collective-permute-done.17 = bf16[512,512]{0,1:T(8,128)(2,1)S(1)} collective-permute-done((bf16[512,512]{0,1:T(8,128)(2,1)}, bf16[512,512]{0,1:T(8,128)(2,1)S(1)}, u32[]{:S(2)}, u32[]{:S(2)}) %collective-permute-start.17) | collective-permute-done | bytes 524320 | tf_op jit(solution)/shard_map/ppermute | solution.py:19
  (216 shorter events, 293.0 us)
Async XLA Ops:
  7.2 73.7 %all-gather.6.cloned.1.call-start = ((), (), s32[]{:S(2)}) async-start(), calls=%async_computation.7 | async-start | bytes 9437184 | tf_op jit(solution)/shard_map/all_gather | solution.py:64
  36.5 310.2 %all-reduce.11.cloned.1.call-start = ((), (), s32[]{:S(2)}) async-start(), calls=%async_computation.3 | async-start | bytes 2097152 | tf_op jit(solution)/shard_map/psum | solution.py:33
  264.5 453.7 %all-reduce.13.cloned.1.call-start = ((), (), s32[]{:S(2)}) async-start(), calls=%async_computation.4 | async-start | bytes 2097152 | tf_op jit(solution)/shard_map/psum | solution.py:33
  355.0 15.5 %collective-permute-start = (bf16[512,512]{0,1:T(8,128)(2,1)S(1)}, bf16[512,512]{0,1:T(8,128)(2,1)S(1)}, u32[]{:S(2)}, u32[]{:S(2)}) collective-permute-start(bf16[512,512]{0,1:T(8,128)(2,1)S(1)} %get-tuple-element.132), channel_id=1, source_target_pairs={{0,1},{1,2},{2,3},{3,4},{4,5},{5,6},{6,7},{7,8},{8,9},{9,10},{10,1... | collective-permute-start | bytes 1572872 | tf_op jit(solution)/shard_map/ppermute | solution.py:19
  356.0 14.5 %collective-permute-start.1 = (bf16[512,512]{0,1:T(8,128)(2,1)S(1)}, bf16[512,512]{0,1:T(8,128)(2,1)S(1)}, u32[]{:S(2)}, u32[]{:S(2)}) collective-permute-start(bf16[512,512]{0,1:T(8,128)(2,1)S(1)} %get-tuple-element.132), channel_id=1, source_target_pairs={{0,15},{1,0},{2,1},{3,2},{4,3},{5,4},{6,5},{7,6},{8,7},{9,8},{10,9... | collective-permute-start | bytes 1572872 | tf_op jit(solution)/shard_map/ppermute | solution.py:24
  370.5 14.5 %collective-permute-start.2 = (bf16[512,512]{0,1:T(8,128)(2,1)S(1)}, bf16[512,512]{0,1:T(8,128)(2,1)S(1)}, u32[]{:S(2)}, u32[]{:S(2)}) collective-permute-start(bf16[512,512]{0,1:T(8,128)(2,1)S(1)} %collective-permute-done), channel_id=1, source_target_pairs={{0,1},{1,2},{2,3},{3,4},{4,5},{5,6},{6,7},{7,8},{8,9},{9,10},{10,1... | collective-permute-start | bytes 1572872 | tf_op jit(solution)/shard_map/ppermute | solution.py:19
  370.5 14.5 %collective-permute-start.3 = (bf16[512,512]{0,1:T(8,128)(2,1)S(1)}, bf16[512,512]{0,1:T(8,128)(2,1)S(1)}, u32[]{:S(2)}, u32[]{:S(2)}) collective-permute-start(bf16[512,512]{0,1:T(8,128)(2,1)S(1)} %collective-permute-done.1), channel_id=1, source_target_pairs={{0,15},{1,0},{2,1},{3,2},{4,3},{5,4},{6,5},{7,6},{8,7},{9,8},{10,9... | collective-permute-start | bytes 1572872 | tf_op jit(solution)/shard_map/ppermute | solution.py:24
  385.1 14.4 %collective-permute-start.5 = (bf16[512,512]{0,1:T(8,128)(2,1)S(1)}, bf16[512,512]{0,1:T(8,128)(2,1)S(1)}, u32[]{:S(2)}, u32[]{:S(2)}) collective-permute-start(bf16[512,512]{0,1:T(8,128)(2,1)S(1)} %collective-permute-done.3), channel_id=1, source_target_pairs={{0,15},{1,0},{2,1},{3,2},{4,3},{5,4},{6,5},{7,6},{8,7},{9,8},{10,9... | collective-permute-start | bytes 1572872 | tf_op jit(solution)/shard_map/ppermute | solution.py:24
  412.2 17.6 %collective-permute-start.9 = (bf16[512,512]{0,1:T(8,128)(2,1)}, bf16[512,512]{0,1:T(8,128)(2,1)}, u32[]{:S(2)}, u32[]{:S(2)}) collective-permute-start(bf16[512,512]{0,1:T(8,128)(2,1)} %collective-permute-done.7), channel_id=1, source_target_pairs={{0,15},{1,0},{2,1},{3,2},{4,3},{5,4},{6,5},{7,6},{8,7},{9,8},{10,9... | collective-permute-start | bytes 1572872 | tf_op jit(solution)/shard_map/ppermute | solution.py:24
  429.8 17.1 %collective-permute-start.11 = (bf16[512,512]{0,1:T(8,128)(2,1)}, bf16[512,512]{0,1:T(8,128)(2,1)S(1)}, u32[]{:S(2)}, u32[]{:S(2)}) collective-permute-start(bf16[512,512]{0,1:T(8,128)(2,1)} %collective-permute-done.9), channel_id=1, source_target_pairs={{0,15},{1,0},{2,1},{3,2},{4,3},{5,4},{6,5},{7,6},{8,7},{9,8},{10,9... | collective-permute-start | bytes 1572872 | tf_op jit(solution)/shard_map/ppermute | solution.py:24
  439.1 15.0 %collective-permute-start.12 = (bf16[512,512]{0,1:T(8,128)(2,1)}, bf16[512,512]{0,1:T(8,128)(2,1)S(1)}, u32[]{:S(2)}, u32[]{:S(2)}) collective-permute-start(bf16[512,512]{0,1:T(8,128)(2,1)} %collective-permute-done.10), channel_id=1, source_target_pairs={{0,1},{1,2},{2,3},{3,4},{4,5},{5,6},{6,7},{7,8},{8,9},{9,10},{10,1... | collective-permute-start | bytes 1572872 | tf_op jit(solution)/shard_map/ppermute | solution.py:19
  493.8 317.9 %all-reduce.15.cloned.1.call-start = ((), (), s32[]{:S(2)}) async-start(), calls=%async_computation.5 | async-start | bytes 524288 | tf_op jit(solution)/shard_map/psum | solution.py:126
  728.4 171.7 %all-reduce.17.cloned.1.call-start = ((), (), s32[]{:S(2)}) async-start(), calls=%async_computation.6 | async-start | bytes 524288 | tf_op jit(solution)/shard_map/psum | solution.py:126
  815.9 174.7 %all-gather.8.cloned.1.call-start = ((), (), s32[]{:S(2)}) async-start(), calls=%async_computation.8 | async-start | bytes 2359296 | tf_op jit(solution)/shard_map/all_gather | solution.py:136
  815.9 88.7 %collective-permute-start.16 = (bf16[512,512]{0,1:T(8,128)(2,1)S(1)}, bf16[512,512]{0,1:T(8,128)(2,1)}, u32[]{:S(2)}, u32[]{:S(2)}) collective-permute-start(bf16[512,512]{0,1:T(8,128)(2,1)S(1)} %get-tuple-element.130), channel_id=1, source_target_pairs={{0,15},{1,0},{2,1},{3,2},{4,3},{5,4},{6,5},{7,6},{8,7},{9,8},{10,9... | collective-permute-start | bytes 1572872 | tf_op jit(solution)/shard_map/ppermute | solution.py:24
  818.7 84.7 %collective-permute-start.15 = (bf16[512,512]{0,1:T(8,128)(2,1)S(1)}, bf16[512,512]{0,1:T(8,128)(2,1)}, u32[]{:S(2)}, u32[]{:S(2)}) collective-permute-start(bf16[512,512]{0,1:T(8,128)(2,1)S(1)} %get-tuple-element.130), channel_id=1, source_target_pairs={{0,1},{1,2},{2,3},{3,4},{4,5},{5,6},{6,7},{7,8},{8,9},{9,10},{10,1... | collective-permute-start | bytes 1572872 | tf_op jit(solution)/shard_map/ppermute | solution.py:19
  903.4 16.0 %collective-permute-start.17 = (bf16[512,512]{0,1:T(8,128)(2,1)}, bf16[512,512]{0,1:T(8,128)(2,1)S(1)}, u32[]{:S(2)}, u32[]{:S(2)}) collective-permute-start(bf16[512,512]{0,1:T(8,128)(2,1)} %collective-permute-done.15), channel_id=1, source_target_pairs={{0,1},{1,2},{2,3},{3,4},{4,5},{5,6},{6,7},{7,8},{8,9},{9,10},{10,1... | collective-permute-start | bytes 1572872 | tf_op jit(solution)/shard_map/ppermute | solution.py:19
  904.6 14.8 %collective-permute-start.18 = (bf16[512,512]{0,1:T(8,128)(2,1)}, bf16[512,512]{0,1:T(8,128)(2,1)S(1)}, u32[]{:S(2)}, u32[]{:S(2)}) collective-permute-start(bf16[512,512]{0,1:T(8,128)(2,1)} %collective-permute-done.16), channel_id=1, source_target_pairs={{0,15},{1,0},{2,1},{3,2},{4,3},{5,4},{6,5},{7,6},{8,7},{9,8},{10,9... | collective-permute-start | bytes 1572872 | tf_op jit(solution)/shard_map/ppermute | solution.py:24
  919.4 14.8 %collective-permute-start.19 = (bf16[512,512]{0,1:T(8,128)(2,1)S(1)}, bf16[512,512]{0,1:T(8,128)(2,1)S(1)}, u32[]{:S(2)}, u32[]{:S(2)}) collective-permute-start(bf16[512,512]{0,1:T(8,128)(2,1)S(1)} %collective-permute-done.17), channel_id=1, source_target_pairs={{0,1},{1,2},{2,3},{3,4},{4,5},{5,6},{6,7},{7,8},{8,9},{9,10},{10,1... | collective-permute-start | bytes 1572872 | tf_op jit(solution)/shard_map/ppermute | solution.py:19
  919.4 14.8 %collective-permute-start.20 = (bf16[512,512]{0,1:T(8,128)(2,1)S(1)}, bf16[512,512]{0,1:T(8,128)(2,1)}, u32[]{:S(2)}, u32[]{:S(2)}) collective-permute-start(bf16[512,512]{0,1:T(8,128)(2,1)S(1)} %collective-permute-done.18), channel_id=1, source_target_pairs={{0,15},{1,0},{2,1},{3,2},{4,3},{5,4},{6,5},{7,6},{8,7},{9,8},{10,9... | collective-permute-start | bytes 1572872 | tf_op jit(solution)/shard_map/ppermute | solution.py:24
  948.2 14.3 %collective-permute-start.23 = (bf16[512,512]{0,1:T(8,128)(2,1)}, bf16[512,512]{0,1:T(8,128)(2,1)}, u32[]{:S(2)}, u32[]{:S(2)}) collective-permute-start(bf16[512,512]{0,1:T(8,128)(2,1)} %collective-permute-done.21), channel_id=1, source_target_pairs={{0,1},{1,2},{2,3},{3,4},{4,5},{5,6},{6,7},{7,8},{8,9},{9,10},{10,1... | collective-permute-start | bytes 1572872 | tf_op jit(solution)/shard_map/ppermute | solution.py:19
  948.9 15.8 %collective-permute-start.24 = (bf16[512,512]{0,1:T(8,128)(2,1)}, bf16[512,512]{0,1:T(8,128)(2,1)}, u32[]{:S(2)}, u32[]{:S(2)}) collective-permute-start(bf16[512,512]{0,1:T(8,128)(2,1)} %collective-permute-done.22), channel_id=1, source_target_pairs={{0,15},{1,0},{2,1},{3,2},{4,3},{5,4},{6,5},{7,6},{8,7},{9,8},{10,9... | collective-permute-start | bytes 1572872 | tf_op jit(solution)/shard_map/ppermute | solution.py:24
  988.5 14.5 %collective-permute-start.29 = (bf16[512,512]{0,1:T(8,128)(2,1)S(1)}, bf16[512,512]{0,1:T(8,128)(2,1)S(1)}, u32[]{:S(2)}, u32[]{:S(2)}) collective-permute-start(bf16[512,512]{0,1:T(8,128)(2,1)S(1)} %collective-permute-done.27), channel_id=1, source_target_pairs={{0,1},{1,2},{2,3},{3,4},{4,5},{5,6},{6,7},{7,8},{8,9},{9,10},{10,1... | collective-permute-start | bytes 1572872 | tf_op jit(solution)/shard_map/ppermute | solution.py:19
  995.9 24.2 %all-to-all-start.2 = ((f32[16,4,128]{2,1,0:T(4,128)}), f32[16,4,128]{2,1,0:T(4,128)S(1)}, u32[]{:S(2)}, u32[]{:S(2)}) async-start(f32[16,4,128]{2,1,0:T(4,128)} %copy.36), calls=%async_computation.2 | async-start | bytes 65536 | tf_op jit(solution)/shard_map/all_to_all | solution.py:141
  (29 other events, 829.0 us)
Sparse Core Ops, SparseCore 0:
  31.4 49.3 all-gather.5
  264.6 82.0 all-reduce.10
  493.9 224.2 all-reduce.12
  728.5 83.1 all-reduce.14
  816.0 84.0 all-reduce.16
  903.5 24.7 all-gather.7
